TPU v7x, 32 devices: a whole 2x2x4 slice. The times are simulated.
32 devices in a mesh: wide: 8 (over z, x), narrow: 4 (over y, core).
Axes of the slice: x: 2, y: 2, z: 4, core: 2. Of those that a mesh axis runs over, the one named last changes fastest.
Arguments:
- states: bfloat16 [256, 262144], P('narrow', 'wide'), may hold values from -6 to 6
- obs_ens: bfloat16 [256, 32768], P('narrow', 'wide'), may hold values from -6 to 6
- obs_value: float32 [32768], P('wide'), may hold values from -6 to 6
- obs_prec: float32 [32768], P('wide'), may hold values from 0.1 to 1
- obs_pick: int32 [32, 1024], P('wide'), may hold values from 0 to 4607, as said below
- taper: float32 [32, 1024], P(('wide', 'narrow')), may hold values from 0.1 to 1
Outputs:
- analysis: bfloat16 [256, 262144], P('narrow', 'wide')
Inputs may be any that keep to these rules, and one draw needn't show every extreme that they name: `obs_pick`: within a region the 1024 rows are distinct.
All inputs are finite; a program needn't handle non-finite values.
Results may differ from a plain program's by a relative error of at most 0.0057.
Values may be sent and summed in bfloat16 or wider, within the bound.
No kernel may reach another device: no remote copies, remote signals or barrier semaphores. Data moves between devices by JAX's collectives and lax.ppermute only.
A program may use at most 64 MiB of HBM per device.

v0:
```python
import jax
import jax.numpy as jnp
from jax import lax
from jax.sharding import PartitionSpec as P

HALO = 256
ITERS = 6


def padded(array, sides, width):
    for axis, dim in sides:
        size, length = (lax.axis_size(axis), array.shape[dim])
        up = [(i, (i + 1) % size) for i in range(size)]
        down = [(j, i) for i, j in up]
        last = lax.slice_in_dim(array, length - width, length, axis=dim)
        leading = lax.slice_in_dim(array, 0, width, axis=dim)
        before = lax.ppermute(last, axis, up)
        after = lax.ppermute(leading, axis, down)
        array = jnp.concatenate([before, array, after], axis=dim)
    return array


def analyse(ensemble, observed, precision, taper_row, regional):
    members = ensemble.shape[0]
    obs_mean = jnp.mean(ensemble, axis=0)
    obs_pert = ensemble - obs_mean
    obs_weight = precision * taper_row
    scaled = (obs_pert * jnp.sqrt(obs_weight)).astype(jnp.bfloat16)
    identity = jnp.eye(members, dtype=jnp.float32)
    gram_sum = lax.dot_general(
        scaled, scaled, (((1,), (1,)), ((), ())), preferred_element_type=jnp.float32
    )
    precision_matrix = gram_sum + (members - 1.0) * identity
    forcing = jnp.dot(
        obs_pert,
        obs_weight * (observed - obs_mean),
        precision=lax.Precision.HIGHEST,
        preferred_element_type=jnp.float32,
    )
    norm_scale = jnp.sqrt(jnp.sum(precision_matrix * precision_matrix))
    current = precision_matrix / norm_scale
    root_iter = identity
    for iteration in range(ITERS):
        middle = 1.5 * identity - 0.5 * jnp.dot(
            root_iter, current, precision=lax.Precision.HIGHEST, preferred_element_type=jnp.float32
        )
        current = jnp.dot(
            current, middle, precision=lax.Precision.HIGHEST, preferred_element_type=jnp.float32
        )
        root_iter = jnp.dot(
            middle, root_iter, precision=lax.Precision.HIGHEST, preferred_element_type=jnp.float32
        )
    inv_root = root_iter / jnp.sqrt(norm_scale)
    inner = jnp.dot(
        inv_root, forcing, precision=lax.Precision.HIGHEST, preferred_element_type=jnp.float32
    )
    mean_weights = jnp.dot(
        inv_root, inner, precision=lax.Precision.HIGHEST, preferred_element_type=jnp.float32
    )
    transform = (jnp.sqrt(members - 1.0) * inv_root + mean_weights[:, None]).astype(jnp.bfloat16)
    state_mean = jnp.mean(regional.astype(jnp.float32), axis=0)
    state_pert = (regional.astype(jnp.float32) - state_mean).astype(jnp.bfloat16)
    mixed = lax.dot_general(
        transform, state_pert, (((0,), (0,)), ((), ())), preferred_element_type=jnp.float32
    )
    return (state_mean + mixed).astype(jnp.bfloat16)


def body(states, obs_ens, obs_value, obs_prec, obs_pick, taper):
    band_regions = lax.axis_size("narrow")
    position = lax.axis_index("narrow")
    members = obs_ens.shape[0] * band_regions
    extended = padded(obs_ens, (("wide", 1),), HALO)
    stat_pair = padded(jnp.stack([obs_value, obs_prec]), (("wide", 1),), HALO)
    own_rows = lax.dynamic_index_in_dim(obs_pick, position, 0, keepdims=False)
    chosen = jnp.take(extended, obs_pick.reshape(-1), axis=1).reshape(
        extended.shape[0], band_regions, -1
    )
    arrived = lax.all_to_all(chosen, "narrow", split_axis=1, concat_axis=0, tiled=True)
    picked = arrived.reshape(members, -1)
    stat_rows = jnp.take(stat_pair, own_rows, axis=1)
    regional = lax.all_to_all(states, "narrow", split_axis=1, concat_axis=0, tiled=True)
    result = analyse(picked.astype(jnp.float32), stat_rows[0], stat_rows[1], taper[0], regional)
    return lax.all_to_all(result, "narrow", split_axis=0, concat_axis=1, tiled=True)


def solution(mesh):
    return jax.shard_map(
        body,
        mesh=mesh,
        in_specs=(
            P("narrow", "wide"),
            P("narrow", "wide"),
            P("wide"),
            P("wide"),
            P("wide", None),
            P(("wide", "narrow"), None),
        ),
        out_specs=P("narrow", "wide"),
        check_vma=False,
    )
```

profile of v0, /device:TPU:0, one launch (start us, length us, event | category | flops | bytes accessed | tf_op | source)
XLA Modules:
  0.0 160.5 jit_solution(12780005530070920755)
XLA Ops:
  0.0 0.7 pad_maximum_fusion.3
  0.7 3.0 %collective-permute-start.2 = (f32[2,256]{1,0:T(2,128)S(1)}, f32[2,256]{1,0:T(2,128)S(1)}, u32[]{:S(2)}, u32[]{:S(2)}) collective-permute-start(f32[2,256]{1,0:T(2,128)S(1)} %get-tuple-element.11), channel_id=1, source_target_pairs={{0,4},{4,8},{8,12},{12,16},{16,20},{20,24},{24,28},{28,0},{1,5},{5... | collective-permute-start | bytes 6152 | tf_op jit(solution)/shard_map/ppermute | solution.py:17
  3.7 3.1 %collective-permute-start.3 = (f32[2,256]{1,0:T(2,128)S(1)}, f32[2,256]{1,0:T(2,128)S(1)}, u32[]{:S(2)}, u32[]{:S(2)}) collective-permute-start(f32[2,256]{1,0:T(2,128)S(1)} %get-tuple-element.12), channel_id=1, source_target_pairs={{4,0},{8,4},{12,8},{16,12},{20,16},{24,20},{28,24},{0,28},{5,1},{9... | collective-permute-start | bytes 6152 | tf_op jit(solution)/shard_map/ppermute | solution.py:18
  6.9 1.5 copy.24
  8.5 4.7 %collective-permute-start.1 = (bf16[64,256]{0,1:T(8,128)(2,1)S(1)}, bf16[64,256]{0,1:T(8,128)(2,1)S(1)}, u32[]{:S(2)}, u32[]{:S(2)}) collective-permute-start(bf16[64,256]{0,1:T(8,128)(2,1)S(1)} %get-tuple-element.10), channel_id=1, source_target_pairs={{4,0},{8,4},{12,8},{16,12},{20,16},{24,20},{28,24},{0,28},{5,1},{9... | collective-permute-start | bytes 98312 | tf_op jit(solution)/shard_map/ppermute | solution.py:18
  13.9 0.7 compare_select_fusion.2
  14.7 0.7 copy.34
  15.4 0.9 copy.29
  16.4 4.6 %copy.36 = bf16[8,4,8,8192]{3,2,0,1:T(8,128)(2,1)} copy(bf16[8,4,8,8192]{3,2,1,0:T(8,128)(2,1)} %bitcast.95) | data formatting | bytes 8388608 | tf_op jit(solution)/shard_map/all_to_all | solution.py:82
  21.3 12.1 %gather_fusion = bf16[4096,64]{1,0:T(8,128)(2,1)S(1)} fusion(bf16[64,4608]{0,1:T(8,128)(2,1)S(1)} %pad_maximum_fusion, s32[4096]{0:T(1024)S(1)} %broadcast_clamp_fusion), kind=kCustom, calls=%fused_computation | custom fusion | bytes 1064960 | tf_op jit(solution)/shard_map/jit(_take)/gather | solution.py:76
  33.7 0.8 broadcast_select_fusion
  34.6 3.5 %all-to-all-start.1 = ((bf16[64,4,1024]{2,0,1:T(8,128)(2,1)}), bf16[64,4,1024]{2,0,1:T(8,128)(2,1)S(1)}, u32[]{:S(2)}, u32[]{:S(2)}) async-start(bf16[64,4,1024]{2,0,1:T(8,128)(2,1)} %broadcast_select_fusion), calls=%async_computation.1 | async-start | bytes 1048576 | tf_op jit(solution)/shard_map/all_to_all | solution.py:79
  38.9 4.0 %gather_fusion.1 = f32[1024,2]{1,0:T(8,128)} fusion(f32[2,4608]{0,1:T(8,128)S(1)} %copy.28, s32[1024]{0:T(1024)S(1)} %broadcast_clamp_fusion.1), kind=kCustom, calls=%fused_computation.1 | custom fusion | bytes 20480 | tf_op jit(solution)/shard_map/jit(_take)/gather | solution.py:81
  42.9 1.2 select_bitcast_fusion
  44.2 2.7 %all-to-all-done.1 = bf16[64,4,1024]{2,0,1:T(8,128)(2,1)S(1)} async-done(((bf16[64,4,1024]{2,0,1:T(8,128)(2,1)}), bf16[64,4,1024]{2,0,1:T(8,128)(2,1)S(1)}, u32[]{:S(2)}, u32[]{:S(2)}) %all-to-all-start.1) | async-done | bytes 524320 | tf_op jit(solution)/shard_map/all_to_all | solution.py:79
  46.8 5.0 %all-to-all-start = ((bf16[64,4,8192]{2,0,1:T(8,128)(2,1)}), bf16[64,4,8192]{2,0,1:T(8,128)(2,1)}, u32[]{:S(2)}, u32[]{:S(2)}) async-start(bf16[64,4,8192]{2,0,1:T(8,128)(2,1)} %bitcast.92), calls=%async_computation | async-start | bytes 8388608 | tf_op jit(solution)/shard_map/all_to_all | solution.py:82
  52.9 1.0 multiply_reduce_fusion
  61.2 0.9 convolution_bitcast_fusion
  62.7 37.2 %all-to-all-done = bf16[64,4,8192]{2,0,1:T(8,128)(2,1)} async-done(((bf16[64,4,8192]{2,0,1:T(8,128)(2,1)}), bf16[64,4,8192]{2,0,1:T(8,128)(2,1)}, u32[]{:S(2)}, u32[]{:S(2)}) %all-to-all-start) | async-done | bytes 4194336 | tf_op jit(solution)/shard_map/all_to_all | solution.py:82
  99.9 2.9 %convert_reduce_fusion = f32[8192]{0:T(1024)S(1)} fusion(bf16[64,4,8192]{2,0,1:T(8,128)(2,1)} %all-to-all-done), kind=kLoop, calls=%fused_computation.7 | loop fusion | flops 4186112 | bytes 4227072 | tf_op jit(solution)/shard_map/reduce_sum | solution.py:61
  102.8 3.3 %fusion.1 = bf16[256,8192]{1,0:T(8,128)(2,1)S(1)} fusion(f32[8192]{0:T(1024)S(1)} %broadcast_multiply_fusion, bf16[64,4,8192]{2,0,1:T(8,128)(2,1)} %all-to-all-done), kind=kLoop, calls=%fused_computation.5 | loop fusion | flops 6291456 | bytes 8421376 | tf_op jit(solution)/shard_map/convert_element_type | solution.py:62
  106.2 1.4 fusion
  107.5 50.7 %all_to_all.41 = bf16[4,64,8192]{2,1,0:T(8,128)(2,1)S(1)} all-to-all(bf16[4,64,8192]{2,1,0:T(8,128)(2,1)S(1)} %bitcast.91), channel_id=1, replica_groups=mesh['wide'=8,'narrow'=4] {'narrow'}, dimensions={0} | all-to-all | bytes 8388608 | tf_op jit(solution)/shard_map/all_to_all | solution.py:84
  158.2 2.3 %copy.33 = bf16[4,8,8,8192]{3,2,0,1:T(8,128)(2,1)} copy(bf16[4,8,8,8192]{3,2,1,0:T(8,128)(2,1)S(1)} %bitcast.93) | data formatting | bytes 8388608 | tf_op jit(solution)/shard_map/all_to_all | solution.py:84
  (45 shorter events, 10.2 us)
Async XLA Ops:
  0.7 37.3 %collective-permute-start.2 = (f32[2,256]{1,0:T(2,128)S(1)}, f32[2,256]{1,0:T(2,128)S(1)}, u32[]{:S(2)}, u32[]{:S(2)}) collective-permute-start(f32[2,256]{1,0:T(2,128)S(1)} %get-tuple-element.11), channel_id=1, source_target_pairs={{0,4},{4,8},{8,12},{12,16},{16,20},{20,24},{24,28},{28,0},{1,5},{5... | collective-permute-start | bytes 6152 | tf_op jit(solution)/shard_map/ppermute | solution.py:17
  3.7 34.3 %collective-permute-start.3 = (f32[2,256]{1,0:T(2,128)S(1)}, f32[2,256]{1,0:T(2,128)S(1)}, u32[]{:S(2)}, u32[]{:S(2)}) collective-permute-start(f32[2,256]{1,0:T(2,128)S(1)} %get-tuple-element.12), channel_id=1, source_target_pairs={{4,0},{8,4},{12,8},{16,12},{20,16},{24,20},{28,24},{0,28},{5,1},{9... | collective-permute-start | bytes 6152 | tf_op jit(solution)/shard_map/ppermute | solution.py:18
  8.4 12.6 %collective-permute-start = (bf16[64,256]{0,1:T(8,128)(2,1)S(1)}, bf16[64,256]{0,1:T(8,128)(2,1)S(1)}, u32[]{:S(2)}, u32[]{:S(2)}) collective-permute-start(bf16[64,256]{0,1:T(8,128)(2,1)S(1)} %get-tuple-element.9), channel_id=1, source_target_pairs={{0,4},{4,8},{8,12},{12,16},{16,20},{20,24},{24,28},{28,0},{1,5},{5... | collective-permute-start | bytes 98312 | tf_op jit(solution)/shard_map/ppermute | solution.py:17
  8.5 12.5 %collective-permute-start.1 = (bf16[64,256]{0,1:T(8,128)(2,1)S(1)}, bf16[64,256]{0,1:T(8,128)(2,1)S(1)}, u32[]{:S(2)}, u32[]{:S(2)}) collective-permute-start(bf16[64,256]{0,1:T(8,128)(2,1)S(1)} %get-tuple-element.10), channel_id=1, source_target_pairs={{4,0},{8,4},{12,8},{16,12},{20,16},{24,20},{28,24},{0,28},{5,1},{9... | collective-permute-start | bytes 98312 | tf_op jit(solution)/shard_map/ppermute | solution.py:18
  21.2 16.8 %copy-start = (f32[4096]{0:T(1024)S(1)}, f32[4096]{0:T(1024)}, u32[]{:S(2)}) copy-start(f32[4096]{0:T(1024)} %param.9) | copy-start | bytes 49156
  21.3 16.8 %copy-start.1 = (f32[4096]{0:T(1024)S(1)}, f32[4096]{0:T(1024)}, u32[]{:S(2)}) copy-start(f32[4096]{0:T(1024)} %param.8) | copy-start | bytes 49156
  34.6 12.3 %all-to-all-start.1 = ((bf16[64,4,1024]{2,0,1:T(8,128)(2,1)}), bf16[64,4,1024]{2,0,1:T(8,128)(2,1)S(1)}, u32[]{:S(2)}, u32[]{:S(2)}) async-start(bf16[64,4,1024]{2,0,1:T(8,128)(2,1)} %broadcast_select_fusion), calls=%async_computation.1 | async-start | bytes 1048576 | tf_op jit(solution)/shard_map/all_to_all | solution.py:79
  46.8 53.1 %all-to-all-start = ((bf16[64,4,8192]{2,0,1:T(8,128)(2,1)}), bf16[64,4,8192]{2,0,1:T(8,128)(2,1)}, u32[]{:S(2)}, u32[]{:S(2)}) async-start(bf16[64,4,8192]{2,0,1:T(8,128)(2,1)} %bitcast.92), calls=%async_computation | async-start | bytes 8388608 | tf_op jit(solution)/shard_map/all_to_all | solution.py:82
where the time goes:
time: 161 us
  blocking collectives  50.7 us (31%)
  waiting for transfers between devices  39.9 us (25%)
  local copies, waits for them, and re-layouts  27.6 us (17%)
  starting transfers between devices  19.4 us (12%)
  other arithmetic  11.7 us (7%)
  matrix products  10.2 us (6%)
    all_to_all x1, blocking collectives, body(): lax.all_to_all(result, 'narrow', split_axis=0, concat_axis=1, tiled=True)  50.7 us
    all_to_all x1, waiting for transfers between devices, body(): lax.all_to_all(states, 'narrow', split_axis=1, concat_axis=0, tiled=True)  37.2 us
    gather x2, local copies, waits for them, and re-layouts, body(): jnp.take(extended, obs_pick.reshape(-1), axis=1)  12.5 us
    ppermute x2, starting transfers between devices, padded(): after = lax.ppermute(leading, axis, down)  7.81 us
    all_to_all x1, starting transfers between devices, body(): lax.all_to_all(states, 'narrow', split_axis=1, concat_axis=0, tiled=True)  5.04 us
    all_to_all x1, local copies, waits for them, and re-layouts, body(): lax.all_to_all(states, 'narrow', split_axis=1, concat_axis=0, tiled=True)  4.64 us
    gather x1, local copies, waits for them, and re-layouts, body(): stat_rows = jnp.take(stat_pair, own_rows, axis=1)  4.04 us
    all_to_all x1, starting transfers between devices, body(): lax.all_to_all(chosen, 'narrow', split_axis=1, concat_axis=0, tiled=True)  3.47 us
  transfers between devices with their start and end apart: 6, of which 2 were waited for; matrix products, arithmetic and copies ran while one was open for 24% of the time, Pallas kernels for 0%

commit v1 on v0

--- a/solution.py
+++ b/solution.py
@@ -79,7 +79,19 @@
     arrived = lax.all_to_all(chosen, "narrow", split_axis=1, concat_axis=0, tiled=True)
     picked = arrived.reshape(members, -1)
     stat_rows = jnp.take(stat_pair, own_rows, axis=1)
-    regional = lax.all_to_all(states, "narrow", split_axis=1, concat_axis=0, tiled=True)
+    ways, here = (lax.axis_size("narrow"), lax.axis_index("narrow"))
+    width_2 = states.shape[1] // ways
+    shape = list(states.shape)
+    shape[1] = width_2
+    height = shape[0]
+    shape[0] = height * ways
+    full = jnp.zeros(shape, states.dtype)
+    for mask in range(ways):
+        part = lax.dynamic_slice_in_dim(states, (here ^ mask) * width_2, width_2, axis=1)
+        if mask:
+            part = lax.ppermute(part, "narrow", [(d, d ^ mask) for d in range(ways)])
+        full = lax.dynamic_update_slice_in_dim(full, part, (here ^ mask) * height, axis=0)
+    regional = full
     result = analyse(picked.astype(jnp.float32), stat_rows[0], stat_rows[1], taper[0], regional)
     return lax.all_to_all(result, "narrow", split_axis=0, concat_axis=1, tiled=True)
 

time: 161 us -> 139 us (0.86)
  waiting for transfers between devices: 39.9 us -> 17.9 us
  local copies, waits for them, and re-layouts: 27.6 us -> 33.3 us
  other arithmetic: 11.7 us -> 6.26 us
  starting transfers between devices: 19.4 us -> 16.6 us
  matrix products: 10.2 us -> 12.4 us
    all_to_all x1 -> x0, waiting for transfers between devices: 37.2 us -> none  [body(): lax.all_to_all(states, 'narrow', split_axis=1, concat_axis=0, tiled=True)]
    all_to_all x1, waiting for transfers between devices: 2.69 us -> 16.4 us  [body(): lax.all_to_all(chosen, 'narrow', split_axis=1, concat_axis=0, tiled=True)]
    dynamic_update_slice x0 -> x3, local copies, waits for them, and re-layouts: none -> 6.85 us  [body(): lax.dynamic_update_slice_in_dim(full, part, (here ^ mask) * height, axis=0)]
    all_to_all x1 -> x0, starting transfers between devices: 5.04 us -> none  [body(): lax.all_to_all(states, 'narrow', split_axis=1, concat_axis=0, tiled=True)]
    all_to_all x1 -> x0, local copies, waits for them, and re-layouts: 4.64 us -> none  [body(): lax.all_to_all(states, 'narrow', split_axis=1, concat_axis=0, tiled=True)]
    convert_element_type x1 -> x0, other arithmetic: 3.35 us -> none  [analyse(): (regional.astype(jnp.float32) - state_mean).astype(jnp.bfloat16)]
    ppermute x0 -> x3, starting transfers between devices: none -> 3.11 us  [body(): part = lax.ppermute(part, 'narrow', [(d, d ^ mask) for d in range(ways)])]
    ppermute x2, starting transfers between devices: 3.07 us -> 0.01 us  [padded(): before = lax.ppermute(last, axis, up)]
  transfers between devices with their start and end apart: 6 -> 8, of which waited for: 2 -> 2; matrix products, arithmetic and copies ran while one was open for 24% -> 25% of each run, Pallas kernels for 0% -> 0%
where the time goes in v1:
time: 139 us
  blocking collectives  51 us (37%)
  local copies, waits for them, and re-layouts  33.3 us (24%)
  waiting for transfers between devices  17.9 us (13%)
  starting transfers between devices  16.6 us (12%)
  matrix products  12.4 us (9%)
  other arithmetic  6.26 us (5%)
    all_to_all x1, blocking collectives, body(): lax.all_to_all(result, 'narrow', split_axis=0, concat_axis=1, tiled=True)  51 us
    all_to_all x1, waiting for transfers between devices, body(): lax.all_to_all(chosen, 'narrow', split_axis=1, concat_axis=0, tiled=True)  16.4 us
    gather x2, local copies, waits for them, and re-layouts, body(): jnp.take(extended, obs_pick.reshape(-1), axis=1)  12.5 us
    ppermute x2, starting transfers between devices, padded(): after = lax.ppermute(leading, axis, down)  9.88 us
    dynamic_update_slice x3, local copies, waits for them, and re-layouts, body(): lax.dynamic_update_slice_in_dim(full, part, (here ^ mask) * height, axis=0)  6.85 us
    gather x1, local copies, waits for them, and re-layouts, body(): stat_rows = jnp.take(stat_pair, own_rows, axis=1)  4.02 us
    dot_general x1, matrix products, analyse(): lax.dot_general(transform, state_pert, (((0,), (0,)), ((), ())), preferre...  3.66 us
    all_to_all x1, starting transfers between devices, body(): lax.all_to_all(chosen, 'narrow', split_axis=1, concat_axis=0, tiled=True)  3.65 us
  transfers between devices with their start and end apart: 8, of which 2 were waited for; matrix products, arithmetic and copies ran while one was open for 25% of the time, Pallas kernels for 0%

profile of v1, /device:TPU:0, one launch (start us, length us, event | category | flops | bytes accessed | tf_op | source)
XLA Modules:
  0.0 138.7 jit_solution(7686517732266846257)
XLA Ops:
  0.0 2.6 %broadcast_in_dim.28 = bf16[256,8192]{1,0:T(8,128)(2,1)} broadcast(bf16[]{:T(256)} %constant.19.clone.1), dimensions={} | broadcast | bytes 4194306 | tf_op jit(solution)/shard_map/broadcast_in_dim | solution.py:88
  2.6 1.1 copy-done
  3.7 2.2 %constant_dynamic-slice_fusion.1 = (bf16[64,8192]{1,0:T(8,128)(2,1)}, bf16[64,8192]{1,0:T(8,128)(2,1)}, bf16[256,8192]{1,0:T(8,128)(2,1)}, bf16[64,8192]{1,0:T(8,128)(2,1)}) fusion(bf16[64,32768]{1,0:T(8,128)(2,1)S(1)} %copy-done, s32[]{:T(128)S(6)} %select_n.76, s32[]{:T(128)S(6)} %select_n.72, bf16[256,8192]{1,0:T(8,128)(2,1)} %broadcast_in_dim.28, ...), kind=kLoop, calls=%fused_computation.57 | loop fusion | bytes 8388628 | tf_op jit(solution)/shard_map/dynamic_slice | solution.py:90
  6.4 2.5 %collective-permute-start.1 = (bf16[64,8192]{1,0:T(8,128)(2,1)}, bf16[64,8192]{1,0:T(8,128)(2,1)}, u32[]{:S(2)}, u32[]{:S(2)}) collective-permute-start(bf16[64,8192]{1,0:T(8,128)(2,1)} %get-tuple-element.12), channel_id=1, source_target_pairs={{0,2},{1,3},{2,0},{3,1},{4,6},{5,7},{6,4},{7,5},{8,10},{9,11},{10,... | collective-permute-start | bytes 3145736 | tf_op jit(solution)/shard_map/ppermute | solution.py:92
  9.5 4.8 %collective-permute-start.4 = (bf16[64,256]{0,1:T(8,128)(2,1)S(1)}, bf16[64,256]{0,1:T(8,128)(2,1)S(1)}, u32[]{:S(2)}, u32[]{:S(2)}) collective-permute-start(bf16[64,256]{0,1:T(8,128)(2,1)S(1)} %get-tuple-element.14), channel_id=1, source_target_pairs={{4,0},{8,4},{12,8},{16,12},{20,16},{24,20},{28,24},{0,28},{5,1},{9... | collective-permute-start | bytes 98312 | tf_op jit(solution)/shard_map/ppermute | solution.py:18
  14.8 1.5 %collective-permute-done.4 = bf16[64,256]{0,1:T(8,128)(2,1)S(1)} collective-permute-done((bf16[64,256]{0,1:T(8,128)(2,1)S(1)}, bf16[64,256]{0,1:T(8,128)(2,1)S(1)}, u32[]{:S(2)}, u32[]{:S(2)}) %collective-permute-start.4) | collective-permute-done | bytes 32800 | tf_op jit(solution)/shard_map/ppermute | solution.py:18
  16.2 5.1 %collective-permute-start.6 = (f32[2,256]{1,0:T(2,128)S(1)}, f32[2,256]{1,0:T(2,128)S(1)}, u32[]{:S(2)}, u32[]{:S(2)}) collective-permute-start(f32[2,256]{1,0:T(2,128)S(1)} %get-tuple-element.16), channel_id=1, source_target_pairs={{4,0},{8,4},{12,8},{16,12},{20,16},{24,20},{28,24},{0,28},{5,1},{9... | collective-permute-start | bytes 6152 | tf_op jit(solution)/shard_map/ppermute | solution.py:18
  21.5 12.1 %gather_fusion = bf16[4096,64]{1,0:T(8,128)(2,1)S(1)} fusion(bf16[64,4608]{0,1:T(8,128)(2,1)S(1)} %pad_maximum_fusion, s32[4096]{0:T(1024)S(1)} %broadcast_clamp_fusion), kind=kCustom, calls=%fused_computation | custom fusion | bytes 1064960 | tf_op jit(solution)/shard_map/jit(_take)/gather | solution.py:76
  34.0 0.9 broadcast_select_fusion
  34.9 3.6 %all-to-all-start = ((bf16[64,4,1024]{2,0,1:T(8,128)(2,1)}), bf16[64,4,1024]{2,0,1:T(8,128)(2,1)S(1)}, u32[]{:S(2)}, u32[]{:S(2)}) async-start(bf16[64,4,1024]{2,0,1:T(8,128)(2,1)} %broadcast_select_fusion), calls=%async_computation | async-start | bytes 1048576 | tf_op jit(solution)/shard_map/all_to_all | solution.py:79
  38.6 0.7 copy.25
  39.3 4.0 %gather_fusion.1 = f32[1024,2]{1,0:T(8,128)} fusion(f32[2,4608]{0,1:T(8,128)S(1)} %copy.25, s32[1024]{0:T(1024)S(1)} %broadcast_clamp_fusion.1), kind=kCustom, calls=%fused_computation.1 | custom fusion | bytes 20480 | tf_op jit(solution)/shard_map/jit(_take)/gather | solution.py:81
  43.4 1.2 select_bitcast_fusion
  44.6 16.4 %all-to-all-done = bf16[64,4,1024]{2,0,1:T(8,128)(2,1)S(1)} async-done(((bf16[64,4,1024]{2,0,1:T(8,128)(2,1)}), bf16[64,4,1024]{2,0,1:T(8,128)(2,1)S(1)}, u32[]{:S(2)}, u32[]{:S(2)}) %all-to-all-start) | async-done | bytes 524320 | tf_op jit(solution)/shard_map/all_to_all | solution.py:79
  61.3 0.6 fusion.13
  62.1 1.0 multiply_reduce_fusion
  70.3 0.9 convolution_bitcast_fusion
  71.8 2.3 %constant_dynamic-update-slice_fusion.2 = bf16[256,8192]{1,0:T(8,128)(2,1)} fusion(bf16[256,8192]{1,0:T(8,128)(2,1)} %get-tuple-element.11, bf16[64,8192]{1,0:T(8,128)(2,1)} %collective-permute-done, s32[]{:T(128)S(6)} %select_n.73), kind=kLoop, calls=%fused_computation.60 | loop fusion | bytes 2097156 | tf_op jit(solution)/shard_map/dynamic_update_slice | solution.py:93
  74.2 2.3 %constant_dynamic-update-slice_fusion.1 = bf16[256,8192]{1,0:T(8,128)(2,1)} fusion(bf16[256,8192]{1,0:T(8,128)(2,1)} %constant_dynamic-update-slice_fusion.2, bf16[64,8192]{1,0:T(8,128)(2,1)} %collective-permute-done.1, s32[]{:T(128)S(6)} %select_n.75), kind=kLoop, calls=%fused_computation.58 | loop fusion | bytes 2097156 | tf_op jit(solution)/shard_map/dynamic_update_slice | solution.py:93
  76.4 2.3 %constant_dynamic-update-slice_fusion = bf16[256,8192]{1,0:T(8,128)(2,1)} fusion(bf16[256,8192]{1,0:T(8,128)(2,1)} %constant_dynamic-update-slice_fusion.1, bf16[64,8192]{1,0:T(8,128)(2,1)} %collective-permute-done.2, s32[]{:T(128)S(6)} %select_n.77), kind=kLoop, calls=%fused_computation.56 | loop fusion | bytes 2097156 | tf_op jit(solution)/shard_map/dynamic_update_slice | solution.py:93
  78.7 2.9 %convert_reduce_fusion = f32[8192]{0:T(1024)S(1)} fusion(bf16[256,8192]{1,0:T(8,128)(2,1)} %constant_dynamic-update-slice_fusion), kind=kLoop, calls=%fused_computation.4 | loop fusion | flops 4186112 | bytes 4227072 | tf_op jit(solution)/shard_map/reduce_sum | solution.py:61
  81.6 3.7 %fusion = bf16[256,8192]{1,0:T(8,128)(2,1)S(1)} fusion(bf16[256,8192]{1,0:T(8,128)(2,1)} %constant_dynamic-update-slice_fusion, f32[8192]{0:T(1024)S(1)} %broadcast_multiply_fusion, f32[256,256]{1,0:T(8,128)S(1)} %convolution_divide_fusion, f32[256]{0:T(256)S(1)} %bitcast.96), kind=kOutput, calls=%fused_computation.5 | convolution fusion | flops 1084424192 | bytes 8684544 | tf_op jit(solution)/shard_map/dot_general | solution.py:63
  85.3 51.0 %all_to_all.28 = bf16[4,64,8192]{2,1,0:T(8,128)(2,1)S(1)} all-to-all(bf16[4,64,8192]{2,1,0:T(8,128)(2,1)S(1)} %bitcast.80), channel_id=1, replica_groups=mesh['wide'=8,'narrow'=4] {'narrow'}, dimensions={0} | all-to-all | bytes 8388608 | tf_op jit(solution)/shard_map/all_to_all | solution.py:96
  136.2 2.5 %copy.29 = bf16[4,8,8,8192]{3,2,0,1:T(8,128)(2,1)} copy(bf16[4,8,8,8192]{3,2,1,0:T(8,128)(2,1)S(1)} %bitcast.81) | data formatting | bytes 8388608 | tf_op jit(solution)/shard_map/all_to_all | solution.py:96
  (60 shorter events, 9.5 us)
Async XLA Ops:
  0.0 3.7 %copy-start = (bf16[64,32768]{1,0:T(8,128)(2,1)S(1)}, bf16[64,32768]{1,0:T(8,128)(2,1)}, u32[]{:S(2)}) copy-start(bf16[64,32768]{1,0:T(8,128)(2,1)} %param.6) | copy-start | bytes 12582916
  3.7 5.3 %copy-start.1 = (bf16[64,4096]{1,0:T(8,128)(2,1)S(1)}, bf16[64,4096]{1,0:T(8,128)(2,1)}, u32[]{:S(2)}) copy-start(bf16[64,4096]{1,0:T(8,128)(2,1)} %param.7) | copy-start | bytes 1572868
  3.7 10.6 %copy-start.2 = (s32[4,1024]{1,0:T(4,128)S(1)}, s32[4,1024]{1,0:T(4,128)}, u32[]{:S(2)}) copy-start(s32[4,1024]{1,0:T(4,128)} %param.10) | copy-start | bytes 49156
  3.7 10.7 %copy-start.3 = (f32[4096]{0:T(1024)S(1)}, f32[4096]{0:T(1024)}, u32[]{:S(2)}) copy-start(f32[4096]{0:T(1024)} %param.9) | copy-start | bytes 49156
  3.7 10.8 %copy-start.4 = (f32[4096]{0:T(1024)S(1)}, f32[4096]{0:T(1024)}, u32[]{:S(2)}) copy-start(f32[4096]{0:T(1024)} %param.8) | copy-start | bytes 49156
  3.7 10.8 %copy-start.5 = (f32[1,1024]{1,0:T(1,128)S(1)}, f32[1,1024]{1,0:T(1,128)}, u32[]{:S(2)}) copy-start(f32[1,1024]{1,0:T(1,128)} %param.11) | copy-start | bytes 12292
  5.9 65.9 %collective-permute-start = (bf16[64,8192]{1,0:T(8,128)(2,1)}, bf16[64,8192]{1,0:T(8,128)(2,1)}, u32[]{:S(2)}, u32[]{:S(2)}) collective-permute-start(bf16[64,8192]{1,0:T(8,128)(2,1)} %get-tuple-element.10), channel_id=1, source_target_pairs={{0,1},{1,0},{2,3},{3,2},{4,5},{5,4},{6,7},{7,6},{8,9},{9,8},{10,11... | collective-permute-start | bytes 3145736 | tf_op jit(solution)/shard_map/ppermute | solution.py:92
  6.4 67.8 %collective-permute-start.1 = (bf16[64,8192]{1,0:T(8,128)(2,1)}, bf16[64,8192]{1,0:T(8,128)(2,1)}, u32[]{:S(2)}, u32[]{:S(2)}) collective-permute-start(bf16[64,8192]{1,0:T(8,128)(2,1)} %get-tuple-element.12), channel_id=1, source_target_pairs={{0,2},{1,3},{2,0},{3,1},{4,6},{5,7},{6,4},{7,5},{8,10},{9,11},{10,... | collective-permute-start | bytes 3145736 | tf_op jit(solution)/shard_map/ppermute | solution.py:92
  8.9 67.5 %collective-permute-start.2 = (bf16[64,8192]{1,0:T(8,128)(2,1)}, bf16[64,8192]{1,0:T(8,128)(2,1)}, u32[]{:S(2)}, u32[]{:S(2)}) collective-permute-start(bf16[64,8192]{1,0:T(8,128)(2,1)} %get-tuple-element.9), channel_id=1, source_target_pairs={{0,3},{1,2},{2,1},{3,0},{4,7},{5,6},{6,5},{7,4},{8,11},{9,10},{10,... | collective-permute-start | bytes 3145736 | tf_op jit(solution)/shard_map/ppermute | solution.py:92
  9.5 6.7 %collective-permute-start.4 = (bf16[64,256]{0,1:T(8,128)(2,1)S(1)}, bf16[64,256]{0,1:T(8,128)(2,1)S(1)}, u32[]{:S(2)}, u32[]{:S(2)}) collective-permute-start(bf16[64,256]{0,1:T(8,128)(2,1)S(1)} %get-tuple-element.14), channel_id=1, source_target_pairs={{4,0},{8,4},{12,8},{16,12},{20,16},{24,20},{28,24},{0,28},{5,1},{9... | collective-permute-start | bytes 98312 | tf_op jit(solution)/shard_map/ppermute | solution.py:18
  14.3 7.0 %collective-permute-start.3 = (bf16[64,256]{0,1:T(8,128)(2,1)S(1)}, bf16[64,256]{0,1:T(8,128)(2,1)S(1)}, u32[]{:S(2)}, u32[]{:S(2)}) collective-permute-start(bf16[64,256]{0,1:T(8,128)(2,1)S(1)} %get-tuple-element.13), channel_id=1, source_target_pairs={{0,4},{4,8},{8,12},{12,16},{16,20},{20,24},{24,28},{28,0},{1,5},{5... | collective-permute-start | bytes 98312 | tf_op jit(solution)/shard_map/ppermute | solution.py:17
  16.2 22.3 %collective-permute-start.6 = (f32[2,256]{1,0:T(2,128)S(1)}, f32[2,256]{1,0:T(2,128)S(1)}, u32[]{:S(2)}, u32[]{:S(2)}) collective-permute-start(f32[2,256]{1,0:T(2,128)S(1)} %get-tuple-element.16), channel_id=1, source_target_pairs={{4,0},{8,4},{12,8},{16,12},{20,16},{24,20},{28,24},{0,28},{5,1},{9... | collective-permute-start | bytes 6152 | tf_op jit(solution)/shard_map/ppermute | solution.py:18
  21.3 17.3 %collective-permute-start.5 = (f32[2,256]{1,0:T(2,128)S(1)}, f32[2,256]{1,0:T(2,128)S(1)}, u32[]{:S(2)}, u32[]{:S(2)}) collective-permute-start(f32[2,256]{1,0:T(2,128)S(1)} %get-tuple-element.15), channel_id=1, source_target_pairs={{0,4},{4,8},{8,12},{12,16},{16,20},{20,24},{24,28},{28,0},{1,5},{5... | collective-permute-start | bytes 6152 | tf_op jit(solution)/shard_map/ppermute | solution.py:17
  34.9 26.1 %all-to-all-start = ((bf16[64,4,1024]{2,0,1:T(8,128)(2,1)}), bf16[64,4,1024]{2,0,1:T(8,128)(2,1)S(1)}, u32[]{:S(2)}, u32[]{:S(2)}) async-start(bf16[64,4,1024]{2,0,1:T(8,128)(2,1)} %broadcast_select_fusion), calls=%async_computation | async-start | bytes 1048576 | tf_op jit(solution)/shard_map/all_to_all | solution.py:79
